TPU v7x, 256 devices: a whole 4x4x8 slice. The times are simulated.
256 devices in a mesh: row: 16 (over x_lo, y, core), col: 16 (over z, x_hi).
Axes of the slice: x: 4 (x_hi: 2, x_lo: 2; x = x_hi * 2 + x_lo), y: 4, z: 8, core: 2. Of those that a mesh axis runs over, the one named last changes fastest.
Arguments:
- block_vecs: float32 [16, 131072], P(None, ('col', 'row')), may hold values from -130 to 130
- direction: float32 [16, 131072], P(None, ('col', 'row')), may hold values from -130 to 130
- blocks: bfloat16 [1024, 32, 128, 128], P('col', 'row'), may hold values from 0 to 4
- block_cols: int32 [1024, 32], P('col', 'row'), may hold values from 0 to 1023, as said below
- live_counts: int32 [1024, 16], P('col', 'row'), may hold values from 1 to 2, as said below
Outputs:
- x_next: float32 [16, 131072], P(None, ('col', 'row'))
- reduced: float32 [48, 48], replicated
- residual: float32 [16, 131072], P(None, ('col', 'row'))
Inputs may be any that keep to these rules, and one draw needn't show every extreme that they name: `block_cols`: A block column index g in slots 2 * r to 2 * r + 1 of any block row satisfies (g // 4) mod 16 == r. `live_counts`: every block row has 2 live slots in at least one segment.
All inputs are finite; a program needn't handle non-finite values.
Results may differ from a plain program's by a relative error of at most 0.0003.
Values sent between devices are 32-bit elements; how exact they have to be, the bound alone decides.
A program may use at most 64 MiB of HBM per device.

v0:
```python
import math
import jax
import jax.numpy as jnp
from jax import lax
from jax.sharding import PartitionSpec as P

highest = lax.Precision.HIGHEST


def outer(left, right):
    return jnp.dot(left, right.T, precision=highest, preferred_element_type=jnp.float32)


def cholesky_lower(matrix):
    order_small = matrix.shape[0]
    places = jnp.arange(order_small, dtype=jnp.int32)

    def column_step(step, lower):
        pick = (places == step).astype(jnp.float32)
        row_now = jnp.sum(lower * pick[:, None], axis=0)
        column_now = jnp.sum(matrix * pick[None, :], axis=1)
        pivot = jnp.sum(column_now * pick) - jnp.sum(row_now * row_now)
        pivot_root = jnp.sqrt(pivot)
        below = (column_now - jnp.sum(lower * row_now[None, :], axis=1)) / pivot_root
        values = jnp.where(places > step, below, jnp.where(places == step, pivot_root, 0.0))
        return lower + values[:, None] * pick[None, :]

    return lax.fori_loop(0, order_small, column_step, jnp.zeros_like(matrix))


def solve_lower(lower, right):
    order_small = lower.shape[0]
    places = jnp.arange(order_small, dtype=jnp.int32)

    def row_step(step, solved):
        pick = (places == step).astype(jnp.float32)
        row_now = jnp.sum(lower * pick[:, None], axis=0)
        pivot = jnp.sum(row_now * pick)
        right_row = jnp.sum(right * pick[:, None], axis=0)
        value = (right_row - jnp.sum(row_now[:, None] * solved, axis=0)) / pivot
        return solved + pick[:, None] * value[None, :]

    return lax.fori_loop(0, order_small, row_step, jnp.zeros_like(right))


def solve_upper_t(lower, right):
    order_small = lower.shape[0]
    places = jnp.arange(order_small, dtype=jnp.int32)

    def row_step(count, solved):
        step = order_small - 1 - count
        pick = (places == step).astype(jnp.float32)
        column_now = jnp.sum(lower * pick[None, :], axis=1)
        pivot = jnp.sum(column_now * pick)
        right_row = jnp.sum(right * pick[:, None], axis=0)
        value = (right_row - jnp.sum(column_now[:, None] * solved, axis=0)) / pivot
        return solved + pick[:, None] * value[None, :]

    return lax.fori_loop(0, order_small, row_step, jnp.zeros_like(right))


def local_layout(block_cols, live_counts, span_rows, block_size, row_count):
    per_span = span_rows // block_size
    span_index = block_cols // per_span
    local_cols = span_index // row_count * per_span + block_cols % per_span
    slot_count = block_cols.shape[1]
    live_mask = (jnp.arange(slot_count, dtype=jnp.int32)[None, :] < live_counts).astype(jnp.float32)
    return (local_cols, live_mask)


def forward_part(col_panel, blocks, local_cols, live_mask):
    vec_width = col_panel.shape[0]
    block_size = blocks.shape[2]
    col_blocks = col_panel.reshape(vec_width, -1, block_size)
    picked = col_blocks[:, local_cols, :] * live_mask[None, :, :, None]
    forward = jnp.einsum(
        "vbkj,bkij->vbi", picked, blocks, precision=highest, preferred_element_type=jnp.float32
    )
    return 0.5 * forward.reshape(vec_width, -1)


def backward_part(row_panel, col_length, blocks, local_cols, live_mask):
    vec_width = row_panel.shape[0]
    block_size = blocks.shape[2]
    row_blocks = row_panel.reshape(vec_width, -1, block_size)
    backward = (
        jnp.einsum(
            "vbi,bkij->vbkj",
            row_blocks,
            blocks,
            precision=highest,
            preferred_element_type=jnp.float32,
        )
        * live_mask[None, :, :, None]
    )
    spread = jnp.zeros((vec_width, col_length // block_size, block_size), jnp.float32)
    spread = spread.at[:, local_cols.reshape(-1), :].add(
        backward.reshape(vec_width, -1, block_size)
    )
    return 0.5 * spread.reshape(vec_width, -1)


def per_device(block_vecs, direction, blocks, block_cols, live_counts):
    row_count = lax.axis_size("row")
    col_count = lax.axis_size("col")
    vec_width = block_vecs.shape[0]
    span_rows = block_vecs.shape[1]
    order_total = span_rows * row_count * col_count
    col_length = span_rows * col_count
    block_size = blocks.shape[2]
    local_cols, live_mask = local_layout(block_cols, live_counts, span_rows, block_size, row_count)
    paired = jnp.concatenate([block_vecs, direction], axis=0)
    pair_cols = lax.all_gather(paired, "col", axis=1, tiled=True)
    pair_rows = lax.all_gather(paired, "row", axis=1, tiled=True)
    forward = forward_part(pair_cols, blocks, local_cols, live_mask)
    backward = backward_part(pair_rows, col_length, blocks, local_cols, live_mask)
    image_pair = lax.psum_scatter(
        forward, "row", scatter_dimension=1, tiled=True
    ) + lax.psum_scatter(backward, "col", scatter_dimension=1, tiled=True)
    image_x = image_pair[:vec_width]
    image_p = image_pair[vec_width:]
    gram_x, cross_x = lax.psum(
        (outer(block_vecs, block_vecs), outer(block_vecs, image_x)), ("row", "col")
    )
    factor_x = cholesky_lower(gram_x)
    coefficient = solve_upper_t(factor_x, solve_lower(factor_x, cross_x))
    resid = image_x - jnp.dot(
        coefficient.T, block_vecs, precision=highest, preferred_element_type=jnp.float32
    )
    basis = jnp.concatenate([block_vecs, resid, direction], axis=0)
    resid_cols = lax.all_gather(resid, "col", axis=1, tiled=True)
    resid_rows = lax.all_gather(resid, "row", axis=1, tiled=True)
    forward_r = forward_part(resid_cols, blocks, local_cols, live_mask)
    column_x = outer(basis, image_x)
    column_p = outer(basis, image_p)
    backward_r = backward_part(resid_rows, col_length, blocks, local_cols, live_mask)
    image_r = lax.psum_scatter(
        forward_r, "row", scatter_dimension=1, tiled=True
    ) + lax.psum_scatter(backward_r, "col", scatter_dimension=1, tiled=True)
    column_r = outer(basis, image_r)
    gram_apply = jnp.concatenate([column_x, column_r, column_p], axis=1)
    gram_basis, gram_apply = lax.psum((outer(basis, basis), gram_apply), ("row", "col"))
    factor = cholesky_lower(gram_basis)
    halfway = solve_lower(factor, 0.5 * (gram_apply + gram_apply.T))
    reduced = solve_lower(factor, halfway.T)
    shifted = reduced + 3.0 * jnp.eye(3 * vec_width, dtype=jnp.float32)
    target = jnp.dot(
        shifted, shifted[:, :vec_width], precision=highest, preferred_element_type=jnp.float32
    )
    mixing = solve_upper_t(factor, target)
    fresh = jnp.dot(mixing.T, basis, precision=highest, preferred_element_type=jnp.float32)
    gram_fresh = lax.psum(outer(fresh, fresh), ("row", "col"))
    factor_fresh = cholesky_lower(gram_fresh)
    x_next = math.sqrt(order_total) * solve_lower(factor_fresh, fresh)
    return (x_next, reduced, resid)


def solution(mesh):
    return jax.shard_map(
        per_device,
        mesh=mesh,
        in_specs=(
            P(None, ("col", "row")),
            P(None, ("col", "row")),
            P("col", "row", None, None),
            P("col", "row"),
            P("col", "row"),
        ),
        out_specs=(P(None, ("col", "row")), P(), P(None, ("col", "row"))),
        check_vma=False,
    )
```

profile of v0, /device:TPU:1, one launch (start us, length us, event | category | flops | bytes accessed | tf_op | source)
XLA Modules:
  0.0 1421.3 jit_solution(11187509048310806808)
XLA Ops:
  11.9 37.2 %all-gather.5.cloned.1.call-done = f32[32,8192]{1,0:T(8,128)} async-done(((f32[32,512]{1,0:T(8,128)}), f32[32,8192]{1,0:T(8,128)}) %all-gather.5.cloned.1.call-update) | async-done | bytes 1048592 | tf_op jit(solution)/shard_map/all_gather | solution.py:114
  49.0 1.4 copy.57
  50.4 4.3 convolution_multiply_fusion
  54.9 5.7 scatter_fusion
  60.6 1.1 copy_bitcast_fusion
  62.0 64.4 %all-gather.3.cloned.1.call-done = f32[32,8192]{1,0:T(8,128)} async-done(((f32[32,512]{1,0:T(8,128)}), f32[32,8192]{1,0:T(8,128)}) %all-gather.3.cloned.1.call-update) | async-done | bytes 1048592 | tf_op jit(solution)/shard_map/all_gather | solution.py:113
  126.4 1.4 copy_bitcast_fusion.2
  128.6 6.0 fusion.45
  134.6 1.1 copy.69
  135.9 192.4 %reduce-scatter.7.cloned.1.call-done = f32[32,512]{1,0:T(8,128)} async-done(((f32[32,8192]{1,0:T(8,128)}), f32[32,512]{1,0:T(8,128)}) %reduce-scatter.7.cloned.1.call-update) | async-done | bytes 65552 | tf_op jit(solution)/shard_map/reduce_scatter | solution.py:119
  328.3 66.4 %reduce-scatter.5.cloned.1.call-done = f32[32,512]{1,0:T(8,128)} async-done(((f32[32,8192]{1,0:T(8,128)}), f32[32,512]{1,0:T(8,128)}) %reduce-scatter.5.cloned.1.call-update) | async-done | bytes 65552 | tf_op jit(solution)/shard_map/reduce_scatter | solution.py:117
  394.7 0.9 add.271
  395.7 78.8 %all-reduce.1 = (f32[16,16]{0,1:T(8,128)S(1)}, f32[16,16]{1,0:T(8,128)S(1)}) all-reduce(f32[16,16]{0,1:T(8,128)S(1)} %convolution_bitcast_fusion.1, f32[16,16]{1,0:T(8,128)S(1)} %fusion.72), channel_id=1, replica_groups=mesh['row'=16,'col'=16] {'row','col'}, use_global_device_ids=true, to_apply=%region_11.12 | all-reduce | flops 512 | bytes 4096 | tf_op jit(solution)/shard_map/psum | solution.py:122
  474.5 37.0 %while.135 = (s32[]{:T(128)}, f32[16,16]{1,0:T(8,128)S(1)}, f32[16,16]{1,0:T(8,128)S(1)}, s32[]{:T(128)}, s32[]{:T(128)}) while((s32[]{:T(128)}, f32[16,16]{1,0:T(8,128)S(1)}, f32[16,16]{1,0:T(8,128)S(1)}, s32[]{:T(128)}, s32[]{:T(128)}) %tuple.302), condition=%wide.region_10.11_spmd.clone.clone, body=%wide.region_4.10_spmd.clone.clone.sunk | while | flops 2978 | bytes 6069 | solution.py:28
  511.6 24.3 %while.129 = (s32[]{:T(128)}, f32[16,16]{1,0:T(8,128)S(1)}, f32[16,16]{1,0:T(8,128)S(1)}, f32[16,16]{1,0:T(8,128)S(1)}, s32[]{:T(128)}, /*index=5*/s32[]{:T(128)}) while((s32[]{:T(128)}, f32[16,16]{1,0:T(8,128)S(1)}, f32[16,16]{1,0:T(8,128)S(1)}, f32[16,16]{1,0:T(8,128)S(1)}, s32[]{:T(128)}, /*index=5*/s32[]{:T(128)}) %tuple.305), condition=%wide.region_17.18_spmd.clone, body=%wide.region_12.17_spmd.clone.sunk | while | flops 2626 | bytes 5984 | solution.py:43
  535.9 24.8 %while.130 = (s32[]{:T(128)}, f32[16,16]{1,0:T(8,128)S(1)}, f32[16,16]{1,0:T(8,128)S(1)}, f32[16,16]{1,0:T(8,128)S(1)}, s32[]{:T(128)}, /*index=5*/s32[]{:T(128)}, s32[]{:T(128)}) while((s32[]{:T(128)}, f32[16,16]{1,0:T(8,128)S(1)}, f32[16,16]{1,0:T(8,128)S(1)}, f32[16,16]{1,0:T(8,128)S(1)}, s32[]{:T(128)}, ...), condition=%wide.region_23.24_spmd.clone, body=%wide.region_18.23_spmd.clone.sunk | while | flops 2627 | bytes 6004 | solution.py:59
  560.9 19.6 %all_gather.15 = f32[16,8192]{1,0:T(8,128)S(1)} all-gather(f32[16,512]{1,0:T(8,128)S(1)} %convolution_subtract_fusion), channel_id=1, replica_groups=mesh['row'=16,'col'=16] {'row'}, dimensions={1}, use_global_device_ids=true | all-gather | bytes 557056 | tf_op jit(solution)/shard_map/all_gather | solution.py:132
  580.6 3.8 convolution_multiply_fusion.1
  584.5 5.2 scatter_fusion.1
  590.6 34.6 %all_gather.14 = f32[16,8192]{1,0:T(8,128)S(1)} all-gather(f32[16,512]{1,0:T(8,128)S(1)} %convolution_subtract_fusion), channel_id=1, replica_groups=mesh['row'=16,'col'=16] {'col'}, dimensions={1}, use_global_device_ids=true | all-gather | bytes 557056 | tf_op jit(solution)/shard_map/all_gather | solution.py:131
  626.0 5.2 fusion.49
  632.8 145.4 %reduce-scatter.11.cloned.1.call-done = f32[16,512]{1,0:T(8,128)} async-done(((f32[16,8192]{1,0:T(8,128)}), f32[16,512]{1,0:T(8,128)}) %reduce-scatter.11.cloned.1.call-update) | async-done | bytes 32784 | tf_op jit(solution)/shard_map/reduce_scatter | solution.py:139
  778.1 65.7 %reduce-scatter.9.cloned.1.call-done = f32[16,512]{1,0:T(8,128)} async-done(((f32[16,8192]{1,0:T(8,128)}), f32[16,512]{1,0:T(8,128)}) %reduce-scatter.9.cloned.1.call-update) | async-done | bytes 32784 | tf_op jit(solution)/shard_map/reduce_scatter | solution.py:137
  843.8 0.9 fusion.58
  844.8 79.4 %all-reduce = (f32[48,48]{0,1:T(8,128)S(1)}, f32[48,48]{1,0:T(8,128)S(1)}) all-reduce(f32[48,48]{0,1:T(8,128)S(1)} %pad_maximum_fusion.1, f32[48,48]{1,0:T(8,128)S(1)} %fusion.70), channel_id=1, replica_groups=mesh['row'=16,'col'=16] {'row','col'}, use_global_device_ids=true, to_apply=%region_35.36 | all-reduce | flops 4608 | bytes 36864 | tf_op jit(solution)/shard_map/psum | solution.py:142
  924.3 111.3 %while.136 = (s32[]{:T(128)}, f32[48,48]{1,0:T(8,128)S(1)}, f32[48,48]{1,0:T(8,128)S(1)}, s32[]{:T(128)}, s32[]{:T(128)}) while((s32[]{:T(128)}, f32[48,48]{1,0:T(8,128)S(1)}, f32[48,48]{1,0:T(8,128)S(1)}, s32[]{:T(128)}, s32[]{:T(128)}) %tuple.311), condition=%wide.region_31.32_spmd.clone.clone, body=%wide.region_25.31_spmd.clone.clone.sunk | while | flops 25826 | bytes 48693 | solution.py:28
  1035.6 79.4 %while.131 = (s32[]{:T(128)}, f32[48,48]{1,0:T(8,128)S(1)}, f32[48,48]{1,0:T(8,128)S(1)}, f32[48,48]{1,0:T(8,128)S(1)}, s32[]{:T(128)}, /*index=5*/s32[]{:T(128)}) while((s32[]{:T(128)}, f32[48,48]{1,0:T(8,128)S(1)}, f32[48,48]{1,0:T(8,128)S(1)}, f32[48,48]{1,0:T(8,128)S(1)}, s32[]{:T(128)}, /*index=5*/s32[]{:T(128)}) %tuple.314), condition=%wide.region_41.42_spmd.clone, body=%wide.region_36.41_spmd.clone.sunk | while | flops 23234 | bytes 48480 | solution.py:43
  1115.1 79.4 %while.132 = (s32[]{:T(128)}, f32[48,48]{1,0:T(8,128)S(1)}, f32[48,48]{1,0:T(8,128)S(1)}, f32[48,48]{1,0:T(8,128)S(1)}, s32[]{:T(128)}, /*index=5*/s32[]{:T(128)}) while((s32[]{:T(128)}, f32[48,48]{1,0:T(8,128)S(1)}, f32[48,48]{1,0:T(8,128)S(1)}, f32[48,48]{1,0:T(8,128)S(1)}, s32[]{:T(128)}, /*index=5*/s32[]{:T(128)}) %tuple.344), condition=%wide.region_47.48_spmd.clone, body=%wide.region_42.47_spmd.clone.sunk | while | flops 23234 | bytes 48480 | solution.py:43
  1194.8 81.8 %while.133 = (s32[]{:T(128)}, f32[48,16]{0,1:T(8,128)S(1)}, f32[48,16]{0,1:T(8,128)S(1)}, f32[48,48]{1,0:T(8,128)S(1)}, s32[]{:T(128)}, /*index=5*/s32[]{:T(128)}, s32[]{:T(128)}) while((s32[]{:T(128)}, f32[48,16]{0,1:T(8,128)S(1)}, f32[48,16]{0,1:T(8,128)S(1)}, f32[48,48]{1,0:T(8,128)S(1)}, s32[]{:T(128)}, ...), condition=%wide.region_53.54_spmd.clone, body=%wide.region_48.53_spmd.clone.sunk | while | flops 10947 | bytes 23348 | solution.py:59
  1276.8 73.6 %psum.39 = f32[16,16]{1,0:T(8,128)S(1)} all-reduce(f32[16,16]{1,0:T(8,128)S(1)} %fusion.73), channel_id=1, replica_groups=mesh['row'=16,'col'=16] {'row','col'}, use_global_device_ids=true, to_apply=%region_54.55 | all-reduce | flops 256 | bytes 2048 | tf_op jit(solution)/shard_map/psum | solution.py:152
  1350.5 37.0 %while.137 = (s32[]{:T(128)}, f32[16,16]{1,0:T(8,128)S(1)}, f32[16,16]{1,0:T(8,128)S(1)}, s32[]{:T(128)}, s32[]{:T(128)}) while((s32[]{:T(128)}, f32[16,16]{1,0:T(8,128)S(1)}, f32[16,16]{1,0:T(8,128)S(1)}, s32[]{:T(128)}, s32[]{:T(128)}) %tuple.323), condition=%wide.region_61.62_spmd.clone.clone, body=%wide.region_55.61_spmd.clone.clone.sunk | while | flops 2978 | bytes 6069 | solution.py:28
  1387.5 26.3 %while.134 = (s32[]{:T(128)}, f32[16,512]{1,0:T(8,128)S(1)}, f32[16,512]{1,0:T(8,128)S(1)}, f32[16,16]{1,0:T(8,128)S(1)}, s32[]{:T(128)}, /*index=5*/s32[]{:T(128)}) while((s32[]{:T(128)}, f32[16,512]{1,0:T(8,128)S(1)}, f32[16,512]{1,0:T(8,128)S(1)}, f32[16,16]{1,0:T(8,128)S(1)}, s32[]{:T(128)}, /*index=5*/s32[]{:T(128)}) %tuple.326), condition=%wide.region_67.68_spmd.clone, body=%wide.region_62.67_spmd.clone.sunk | while | flops 66114 | bytes 144928 | solution.py:43
  (1698 shorter events, 405.3 us)
Async XLA Ops:
  7.2 41.9 %all-gather.5.cloned.1.call-start = ((), (), s32[]{:S(2)}) async-start(), calls=%async_computation.6 | async-start | bytes 1114112 | tf_op jit(solution)/shard_map/all_gather | solution.py:114
  8.7 0.6 copy-start.4
  9.4 117.1 %all-gather.3.cloned.1.call-start = ((), (), s32[]{:S(2)}) async-start(), calls=%async_computation.4 | async-start | bytes 1114112 | tf_op jit(solution)/shard_map/all_gather | solution.py:113
  10.1 318.2 %reduce-scatter.7.cloned.1.call-start = ((), (), s32[]{:S(2)}) async-start(), calls=%async_computation.7 | async-start | bytes 1114112 | tf_op jit(solution)/shard_map/reduce_scatter | solution.py:119
  61.7 333.0 %reduce-scatter.5.cloned.1.call-start = ((), (), s32[]{:S(2)}) async-start(), calls=%async_computation.5 | async-start | bytes 1114112 | tf_op jit(solution)/shard_map/reduce_scatter | solution.py:117
  134.6 1.2 copy-start.1
  135.7 642.4 %reduce-scatter.11.cloned.1.call-start = ((), (), s32[]{:S(2)}) async-start(), calls=%async_computation.9 | async-start | bytes 557056 | tf_op jit(solution)/shard_map/reduce_scatter | solution.py:139
  560.9 715.6 %copy-start.2 = (f32[16,512]{1,0:T(8,128)}, f32[16,512]{1,0:T(8,128)S(1)}, u32[]{:S(2)}) copy-start(f32[16,512]{1,0:T(8,128)S(1)} %convolution_subtract_fusion) | copy-start | bytes 98308
  590.5 253.3 %reduce-scatter.9.cloned.1.call-start = ((), (), s32[]{:S(2)}) async-start(), calls=%async_computation.8 | async-start | bytes 557056 | tf_op jit(solution)/shard_map/reduce_scatter | solution.py:137
  626.0 6.1 copy-start.3
  1194.5 219.9 %copy-start = (f32[48,48]{1,0:T(8,128)}, f32[48,48]{1,0:T(8,128)S(1)}, u32[]{:S(2)}) copy-start(f32[48,48]{1,0:T(8,128)S(1)} %get-tuple-element.811) | copy-start | bytes 27652
Sparse Core Ops, SparseCore 0:
  9.8 39.1 all-gather.4
  51.6 74.7 all-gather.2
  130.3 198.0 reduce-scatter.6
  330.7 63.9 reduce-scatter.4
  590.6 187.4 reduce-scatter.10
  780.5 63.2 reduce-scatter.8
where the time goes:
time: 1430 us; the launch traced here: 1420 us
  waiting for transfers between devices  572 us (40%)
  other arithmetic  410 us (29%)
  blocking collectives  286 us (20%)
  loops' own time  107 us (7%)
  matrix products  21.8 us (2%)
  between operations  14.4 us (1%)
    reduce_scatter x1, waiting for transfers between devices, per_device(): lax.psum_scatter(backward, 'col', scatter_dimension=1, tiled=True)  192 us
    reduce_scatter x1, waiting for transfers between devices, per_device(): lax.psum_scatter(backward_r, 'col', scatter_dimension=1, tiled=True)  145 us
    another operation x3, loops' own time, cholesky_lower(): return lax.fori_loop(0, order_small, column_step, jnp.zeros_like(matrix))  105 us
    div x128, other arithmetic, row_step(): value = (right_row - jnp.sum(row_now[:, None] * solved, axis=0)) / pivot  87.9 us
    reduce_sum x128, other arithmetic, row_step(): pivot = jnp.sum(row_now * pick)  85.7 us
    psum x1, blocking collectives, per_device(): lax.psum((outer(basis, basis), gram_apply), ('row', 'col'))  79.4 us
    psum x1, blocking collectives, per_device(): lax.psum((outer(block_vecs, block_vecs), outer(block_vecs, image_x)), ('r...  78.8 us
    psum x1, blocking collectives, per_device(): gram_fresh = lax.psum(outer(fresh, fresh), ('row', 'col'))  73.6 us
  transfers between devices with their start and end apart: 6, of which 6 were waited for; matrix products, arithmetic and copies ran while one was open for 2% of the time, Pallas kernels for 0%

commit v1 on v0

--- a/solution.py
+++ b/solution.py
@@ -120,7 +120,7 @@
     image_x = image_pair[:vec_width]
     image_p = image_pair[vec_width:]
     gram_x, cross_x = lax.psum(
-        (outer(block_vecs, block_vecs), outer(block_vecs, image_x)), ("row", "col")
+        lax.psum((outer(block_vecs, block_vecs), outer(block_vecs, image_x)), "col"), "row"
     )
     factor_x = cholesky_lower(gram_x)
     coefficient = solve_upper_t(factor_x, solve_lower(factor_x, cross_x))

time: 1430 us -> 1480 us (1.035)
  blocking collectives: 286 us -> 337 us
    psum x1 -> x2, blocking collectives: 78.8 us -> 129 us  [the longest x1 66.3 us: per_device(): lax.psum(lax.psum((outer(block_vecs, block_vecs), outer(block_vecs, image...]
where the time goes in v1:
time: 1480 us; the launch traced here: 1470 us
  waiting for transfers between devices  574 us (39%)
  other arithmetic  410 us (28%)
  blocking collectives  337 us (23%)
  loops' own time  107 us (7%)
  matrix products  21.8 us (1%)
    reduce_scatter x1, waiting for transfers between devices, per_device(): lax.psum_scatter(backward, 'col', scatter_dimension=1, tiled=True)  192 us
    reduce_scatter x1, waiting for transfers between devices, per_device(): lax.psum_scatter(backward_r, 'col', scatter_dimension=1, tiled=True)  147 us
    another operation x3, loops' own time, cholesky_lower(): return lax.fori_loop(0, order_small, column_step, jnp.zeros_like(matrix))  105 us
    div x128, other arithmetic, row_step(): value = (right_row - jnp.sum(row_now[:, None] * solved, axis=0)) / pivot  87.9 us
    reduce_sum x128, other arithmetic, row_step(): pivot = jnp.sum(row_now * pick)  85.7 us
    psum x1, blocking collectives, per_device(): lax.psum((outer(basis, basis), gram_apply), ('row', 'col'))  79.4 us
    psum x1, blocking collectives, per_device(): gram_fresh = lax.psum(outer(fresh, fresh), ('row', 'col'))  73.6 us
    reduce_scatter x1, waiting for transfers between devices, per_device(): lax.psum_scatter(forward, 'row', scatter_dimension=1, tiled=True)  66.4 us
  transfers between devices with their start and end apart: 6, of which 6 were waited for; matrix products, arithmetic and copies ran while one was open for 2% of the time, Pallas kernels for 0%

profile of v1, /device:TPU:1, one launch (start us, length us, event | category | flops | bytes accessed | tf_op | source)
XLA Modules:
  0.0 1473.7 jit_solution(2716898674604223993)
XLA Ops:
  11.9 37.2 %all-gather.5.cloned.1.call-done = f32[32,8192]{1,0:T(8,128)} async-done(((f32[32,512]{1,0:T(8,128)}), f32[32,8192]{1,0:T(8,128)}) %all-gather.5.cloned.1.call-update) | async-done | bytes 1048592 | tf_op jit(solution)/shard_map/all_gather | solution.py:114
  49.0 1.4 copy.57
  50.4 4.3 convolution_multiply_fusion
  54.9 5.7 scatter_fusion
  60.6 1.1 copy_bitcast_fusion
  62.0 64.4 %all-gather.3.cloned.1.call-done = f32[32,8192]{1,0:T(8,128)} async-done(((f32[32,512]{1,0:T(8,128)}), f32[32,8192]{1,0:T(8,128)}) %all-gather.3.cloned.1.call-update) | async-done | bytes 1048592 | tf_op jit(solution)/shard_map/all_gather | solution.py:113
  126.4 1.4 copy_bitcast_fusion.2
  128.6 6.0 fusion.45
  134.6 1.1 copy.69
  135.9 192.4 %reduce-scatter.7.cloned.1.call-done = f32[32,512]{1,0:T(8,128)} async-done(((f32[32,8192]{1,0:T(8,128)}), f32[32,512]{1,0:T(8,128)}) %reduce-scatter.7.cloned.1.call-update) | async-done | bytes 65552 | tf_op jit(solution)/shard_map/reduce_scatter | solution.py:119
  328.3 66.4 %reduce-scatter.5.cloned.1.call-done = f32[32,512]{1,0:T(8,128)} async-done(((f32[32,8192]{1,0:T(8,128)}), f32[32,512]{1,0:T(8,128)}) %reduce-scatter.5.cloned.1.call-update) | async-done | bytes 65552 | tf_op jit(solution)/shard_map/reduce_scatter | solution.py:117
  395.7 63.1 %all-reduce.1 = (f32[16,16]{0,1:T(8,128)S(1)}, f32[16,16]{1,0:T(8,128)S(1)}) all-reduce(f32[16,16]{0,1:T(8,128)S(1)} %convolution_bitcast_fusion.1, f32[16,16]{1,0:T(8,128)S(1)} %fusion.72), channel_id=1, replica_groups=mesh['row'=16,'col'=16] {'col'}, use_global_device_ids=true, to_apply=%region_12.13 | all-reduce | flops 512 | bytes 4096 | tf_op jit(solution)/shard_map/psum | solution.py:123
  458.8 66.3 %all-reduce.2 = (f32[16,16]{0,1:T(8,128)S(1)}, f32[16,16]{1,0:T(8,128)S(1)}) all-reduce(f32[16,16]{0,1:T(8,128)S(1)} %get-tuple-element.1100, f32[16,16]{1,0:T(8,128)S(1)} %get-tuple-element.1101), channel_id=1, replica_groups=mesh['row'=16,'col'=16] {'row'}, use_global_device_ids=true, to_apply=%region_13.14 | all-reduce | flops 512 | bytes 4096 | tf_op jit(solution)/shard_map/psum | solution.py:122
  525.2 37.0 %while.135 = (s32[]{:T(128)}, f32[16,16]{1,0:T(8,128)S(1)}, f32[16,16]{1,0:T(8,128)S(1)}, s32[]{:T(128)}, s32[]{:T(128)}) while((s32[]{:T(128)}, f32[16,16]{1,0:T(8,128)S(1)}, f32[16,16]{1,0:T(8,128)S(1)}, s32[]{:T(128)}, s32[]{:T(128)}) %tuple.302), condition=%wide.region_11.12_spmd.clone.clone, body=%wide.region_5.11_spmd.clone.clone.sunk | while | flops 2978 | bytes 6069 | solution.py:28
  562.3 24.3 %while.129 = (s32[]{:T(128)}, f32[16,16]{1,0:T(8,128)S(1)}, f32[16,16]{1,0:T(8,128)S(1)}, f32[16,16]{1,0:T(8,128)S(1)}, s32[]{:T(128)}, /*index=5*/s32[]{:T(128)}) while((s32[]{:T(128)}, f32[16,16]{1,0:T(8,128)S(1)}, f32[16,16]{1,0:T(8,128)S(1)}, f32[16,16]{1,0:T(8,128)S(1)}, s32[]{:T(128)}, /*index=5*/s32[]{:T(128)}) %tuple.305), condition=%wide.region_19.20_spmd.clone, body=%wide.region_14.19_spmd.clone.sunk | while | flops 2626 | bytes 5984 | solution.py:43
  586.5 24.8 %while.130 = (s32[]{:T(128)}, f32[16,16]{1,0:T(8,128)S(1)}, f32[16,16]{1,0:T(8,128)S(1)}, f32[16,16]{1,0:T(8,128)S(1)}, s32[]{:T(128)}, /*index=5*/s32[]{:T(128)}, s32[]{:T(128)}) while((s32[]{:T(128)}, f32[16,16]{1,0:T(8,128)S(1)}, f32[16,16]{1,0:T(8,128)S(1)}, f32[16,16]{1,0:T(8,128)S(1)}, s32[]{:T(128)}, ...), condition=%wide.region_25.26_spmd.clone, body=%wide.region_20.25_spmd.clone.sunk | while | flops 2627 | bytes 6004 | solution.py:59
  611.6 21.8 %all_gather.15 = f32[16,8192]{1,0:T(8,128)S(1)} all-gather(f32[16,512]{1,0:T(8,128)S(1)} %convolution_subtract_fusion), channel_id=1, replica_groups=mesh['row'=16,'col'=16] {'row'}, dimensions={1}, use_global_device_ids=true | all-gather | bytes 557056 | tf_op jit(solution)/shard_map/all_gather | solution.py:132
  633.5 3.8 convolution_multiply_fusion.1
  637.4 5.2 scatter_fusion.1
  643.5 32.5 %all_gather.14 = f32[16,8192]{1,0:T(8,128)S(1)} all-gather(f32[16,512]{1,0:T(8,128)S(1)} %convolution_subtract_fusion), channel_id=1, replica_groups=mesh['row'=16,'col'=16] {'col'}, dimensions={1}, use_global_device_ids=true | all-gather | bytes 557056 | tf_op jit(solution)/shard_map/all_gather | solution.py:131
  676.8 5.2 fusion.49
  683.5 147.0 %reduce-scatter.11.cloned.1.call-done = f32[16,512]{1,0:T(8,128)} async-done(((f32[16,8192]{1,0:T(8,128)}), f32[16,512]{1,0:T(8,128)}) %reduce-scatter.11.cloned.1.call-update) | async-done | bytes 32784 | tf_op jit(solution)/shard_map/reduce_scatter | solution.py:139
  830.5 65.7 %reduce-scatter.9.cloned.1.call-done = f32[16,512]{1,0:T(8,128)} async-done(((f32[16,8192]{1,0:T(8,128)}), f32[16,512]{1,0:T(8,128)}) %reduce-scatter.9.cloned.1.call-update) | async-done | bytes 32784 | tf_op jit(solution)/shard_map/reduce_scatter | solution.py:137
  896.2 0.9 fusion.58
  897.2 79.4 %all-reduce = (f32[48,48]{0,1:T(8,128)S(1)}, f32[48,48]{1,0:T(8,128)S(1)}) all-reduce(f32[48,48]{0,1:T(8,128)S(1)} %pad_maximum_fusion.1, f32[48,48]{1,0:T(8,128)S(1)} %fusion.70), channel_id=1, replica_groups=mesh['row'=16,'col'=16] {'row','col'}, use_global_device_ids=true, to_apply=%region_37.38 | all-reduce | flops 4608 | bytes 36864 | tf_op jit(solution)/shard_map/psum | solution.py:142
  976.8 111.3 %while.136 = (s32[]{:T(128)}, f32[48,48]{1,0:T(8,128)S(1)}, f32[48,48]{1,0:T(8,128)S(1)}, s32[]{:T(128)}, s32[]{:T(128)}) while((s32[]{:T(128)}, f32[48,48]{1,0:T(8,128)S(1)}, f32[48,48]{1,0:T(8,128)S(1)}, s32[]{:T(128)}, s32[]{:T(128)}) %tuple.311), condition=%wide.region_33.34_spmd.clone.clone, body=%wide.region_27.33_spmd.clone.clone.sunk | while | flops 25826 | bytes 48693 | solution.py:28
  1088.0 79.4 %while.131 = (s32[]{:T(128)}, f32[48,48]{1,0:T(8,128)S(1)}, f32[48,48]{1,0:T(8,128)S(1)}, f32[48,48]{1,0:T(8,128)S(1)}, s32[]{:T(128)}, /*index=5*/s32[]{:T(128)}) while((s32[]{:T(128)}, f32[48,48]{1,0:T(8,128)S(1)}, f32[48,48]{1,0:T(8,128)S(1)}, f32[48,48]{1,0:T(8,128)S(1)}, s32[]{:T(128)}, /*index=5*/s32[]{:T(128)}) %tuple.314), condition=%wide.region_43.44_spmd.clone, body=%wide.region_38.43_spmd.clone.sunk | while | flops 23234 | bytes 48480 | solution.py:43
  1167.5 79.4 %while.132 = (s32[]{:T(128)}, f32[48,48]{1,0:T(8,128)S(1)}, f32[48,48]{1,0:T(8,128)S(1)}, f32[48,48]{1,0:T(8,128)S(1)}, s32[]{:T(128)}, /*index=5*/s32[]{:T(128)}) while((s32[]{:T(128)}, f32[48,48]{1,0:T(8,128)S(1)}, f32[48,48]{1,0:T(8,128)S(1)}, f32[48,48]{1,0:T(8,128)S(1)}, s32[]{:T(128)}, /*index=5*/s32[]{:T(128)}) %tuple.344), condition=%wide.region_49.50_spmd.clone, body=%wide.region_44.49_spmd.clone.sunk | while | flops 23234 | bytes 48480 | solution.py:43
  1247.2 81.8 %while.133 = (s32[]{:T(128)}, f32[48,16]{0,1:T(8,128)S(1)}, f32[48,16]{0,1:T(8,128)S(1)}, f32[48,48]{1,0:T(8,128)S(1)}, s32[]{:T(128)}, /*index=5*/s32[]{:T(128)}, s32[]{:T(128)}) while((s32[]{:T(128)}, f32[48,16]{0,1:T(8,128)S(1)}, f32[48,16]{0,1:T(8,128)S(1)}, f32[48,48]{1,0:T(8,128)S(1)}, s32[]{:T(128)}, ...), condition=%wide.region_55.56_spmd.clone, body=%wide.region_50.55_spmd.clone.sunk | while | flops 10947 | bytes 23348 | solution.py:59
  1329.3 73.6 %psum.55 = f32[16,16]{1,0:T(8,128)S(1)} all-reduce(f32[16,16]{1,0:T(8,128)S(1)} %fusion.73), channel_id=1, replica_groups=mesh['row'=16,'col'=16] {'row','col'}, use_global_device_ids=true, to_apply=%region_56.57 | all-reduce | flops 256 | bytes 2048 | tf_op jit(solution)/shard_map/psum | solution.py:152
  1402.9 37.0 %while.137 = (s32[]{:T(128)}, f32[16,16]{1,0:T(8,128)S(1)}, f32[16,16]{1,0:T(8,128)S(1)}, s32[]{:T(128)}, s32[]{:T(128)}) while((s32[]{:T(128)}, f32[16,16]{1,0:T(8,128)S(1)}, f32[16,16]{1,0:T(8,128)S(1)}, s32[]{:T(128)}, s32[]{:T(128)}) %tuple.323), condition=%wide.region_63.64_spmd.clone.clone, body=%wide.region_57.63_spmd.clone.clone.sunk | while | flops 2978 | bytes 6069 | solution.py:28
  1439.9 26.3 %while.134 = (s32[]{:T(128)}, f32[16,512]{1,0:T(8,128)S(1)}, f32[16,512]{1,0:T(8,128)S(1)}, f32[16,16]{1,0:T(8,128)S(1)}, s32[]{:T(128)}, /*index=5*/s32[]{:T(128)}) while((s32[]{:T(128)}, f32[16,512]{1,0:T(8,128)S(1)}, f32[16,512]{1,0:T(8,128)S(1)}, f32[16,16]{1,0:T(8,128)S(1)}, s32[]{:T(128)}, /*index=5*/s32[]{:T(128)}) %tuple.326), condition=%wide.region_69.70_spmd.clone, body=%wide.region_64.69_spmd.clone.sunk | while | flops 66114 | bytes 144928 | solution.py:43
  (1699 shorter events, 406.2 us)
Async XLA Ops:
  7.2 41.9 %all-gather.5.cloned.1.call-start = ((), (), s32[]{:S(2)}) async-start(), calls=%async_computation.6 | async-start | bytes 1114112 | tf_op jit(solution)/shard_map/all_gather | solution.py:114
  8.7 0.6 copy-start.4
  9.4 117.1 %all-gather.3.cloned.1.call-start = ((), (), s32[]{:S(2)}) async-start(), calls=%async_computation.4 | async-start | bytes 1114112 | tf_op jit(solution)/shard_map/all_gather | solution.py:113
  10.1 318.2 %reduce-scatter.7.cloned.1.call-start = ((), (), s32[]{:S(2)}) async-start(), calls=%async_computation.7 | async-start | bytes 1114112 | tf_op jit(solution)/shard_map/reduce_scatter | solution.py:119
  61.7 333.0 %reduce-scatter.5.cloned.1.call-start = ((), (), s32[]{:S(2)}) async-start(), calls=%async_computation.5 | async-start | bytes 1114112 | tf_op jit(solution)/shard_map/reduce_scatter | solution.py:117
  134.6 1.2 copy-start.1
  135.7 694.8 %reduce-scatter.11.cloned.1.call-start = ((), (), s32[]{:S(2)}) async-start(), calls=%async_computation.9 | async-start | bytes 557056 | tf_op jit(solution)/shard_map/reduce_scatter | solution.py:139
  611.6 717.4 %copy-start.2 = (f32[16,512]{1,0:T(8,128)}, f32[16,512]{1,0:T(8,128)S(1)}, u32[]{:S(2)}) copy-start(f32[16,512]{1,0:T(8,128)S(1)} %convolution_subtract_fusion) | copy-start | bytes 98308
  643.4 252.8 %reduce-scatter.9.cloned.1.call-start = ((), (), s32[]{:S(2)}) async-start(), calls=%async_computation.8 | async-start | bytes 557056 | tf_op jit(solution)/shard_map/reduce_scatter | solution.py:137
  676.8 6.1 copy-start.3
  1247.0 219.9 %copy-start = (f32[48,48]{1,0:T(8,128)}, f32[48,48]{1,0:T(8,128)S(1)}, u32[]{:S(2)}) copy-start(f32[48,48]{1,0:T(8,128)S(1)} %get-tuple-element.811) | copy-start | bytes 27652
Sparse Core Ops, SparseCore 0:
  9.8 39.1 all-gather.4
  51.6 74.7 all-gather.2
  130.3 198.0 reduce-scatter.6
  330.7 63.9 reduce-scatter.4
  643.5 186.9 reduce-scatter.10
  832.9 63.3 reduce-scatter.8
